TPU v7x, 32 devices: a whole 2x2x4 slice. The times are simulated.
32 devices in a mesh: space: 4 (over z), chan: 8 (over y, x, core).
Axes of the slice: x: 2, y: 2, z: 4, core: 2. Of those that a mesh axis runs over, the one named last changes fastest.
Arguments:
- inputs: bfloat16 [1024, 8, 128], P('chan', 'space'), may hold values from -6 to 6
- conv_out: bfloat16 [1024, 8, 128], P('chan', 'space'), may hold values from -90 to 90
- upstream: bfloat16 [1024, 8, 128], P('chan', 'space'), may hold values from -100 to 100
- weights: bfloat16 [27, 1024, 1024], P(None, 'chan'), may hold values from -0.0390625 to 0.0390625
- norm_gain: float32 [1024], P('chan'), may hold values from 0.5 to 2
- run_sigma: float32 [1024], P('chan'), may hold values from 0.3 to 30
Outputs:
- input_grad: bfloat16 [1024, 8, 128], P('chan', 'space')
- weight_grad: float32 [27, 1024, 1024], P(None, 'chan', 'space')
All inputs are finite; a program needn't handle non-finite values.
Results may differ from a plain program's by a relative error of at most 0.005.
Values may be sent and summed in bfloat16 or wider, within the bound.
A program may use at most 128 MiB of HBM per device.

v0:
```python
import jax
import jax.numpy as jnp
from jax import lax
from jax.sharding import PartitionSpec as P

H = 8
W = 16


epsilon = 1e-05
clip_limit = 3.0
taps_list = [(tap // 9, tap // 3 % 3, tap % 3) for tap in range(27)]


def with_halo(cells, sides, width):
    for axis, dim in sides:
        count = lax.axis_size(axis)
        ends = count - 1
        head = lax.slice_in_dim(cells, 0, width, axis=dim)
        tail = lax.slice_in_dim(cells, cells.shape[dim] - width, cells.shape[dim], axis=dim)
        cells = jnp.concatenate(
            [
                lax.ppermute(tail, axis, [(i, (i + 1) % count) for i in range(ends)]),
                cells,
                lax.ppermute(head, axis, [((i + 1) % count, i) for i in range(ends)]),
            ],
            axis=dim,
        )
    return cells


def spread(field):
    shaped = field.reshape(field.shape[0], field.shape[1], H, W)
    return jnp.pad(shaped, ((0, 0), (0, 0), (1, 1), (1, 1)))


def tap_cut(padded, depth_from, row_from, col_from, planes):
    window = padded[
        :, depth_from : depth_from + planes, row_from : row_from + H, col_from : col_from + W
    ]
    return window.reshape(padded.shape[0], planes * H * W)


def input_terms(grad_rows, weight_rows, planes):
    padded = spread(grad_rows)
    total = jnp.zeros((weight_rows.shape[1], planes * H * W), jnp.float32)
    for depth_off, row_off, col_off in taps_list:
        tap_index = 9 * depth_off + 3 * row_off + col_off
        shifted = tap_cut(padded, 2 - depth_off, 2 - row_off, 2 - col_off, planes)
        total = total + jnp.dot(weight_rows[tap_index], shifted, preferred_element_type=jnp.float32)
    return total


def on_device(inputs, conv_out, upstream, weights, norm_gain, run_sigma):
    channels, planes, plane_len = inputs.shape
    cells_total = planes * plane_len * lax.axis_size("space")
    outputs_f = conv_out.astype(jnp.float32)
    scaled = upstream.astype(jnp.float32) * norm_gain[:, None, None]
    mean_val = lax.psum(jnp.sum(outputs_f, axis=(1, 2)), "space") / cells_total
    centred = outputs_f - mean_val[:, None, None]
    var_val = lax.psum(jnp.sum(centred * centred, axis=(1, 2)), "space") / cells_total
    std_dev = jnp.sqrt(var_val + epsilon)
    normed = centred / std_dev[:, None, None]
    total_up, total_cross = lax.psum(
        (jnp.sum(scaled, axis=(1, 2)), jnp.sum(scaled * normed, axis=(1, 2))), "space"
    )
    mean_up = total_up / cells_total
    mean_cross = total_cross / cells_total
    ratios = jnp.clip(std_dev / run_sigma, 1.0 / clip_limit, clip_limit)
    out_grad = (
        (ratios / std_dev)[:, None, None]
        * (scaled - mean_up[:, None, None] - normed * mean_cross[:, None, None])
    ).astype(jnp.bfloat16)
    grad_rim = with_halo(out_grad, (("space", 1),), 1)
    full_grad = lax.all_gather(grad_rim, "chan", axis=0, tiled=True)
    input_acc = input_terms(full_grad, weights, planes)
    input_rim = with_halo(inputs, (("space", 1),), 1)
    input_pad = spread(input_rim)
    input_shift = jnp.stack(
        [
            tap_cut(input_pad, depth_off, row_off, col_off, planes)
            for depth_off, row_off, col_off in taps_list
        ]
    )
    inner = full_grad[:, 1 : planes + 1].reshape(full_grad.shape[0], planes * plane_len)
    weight_acc = jnp.einsum("kin,mn->kim", input_shift, inner, preferred_element_type=jnp.float32)
    weight_grad = lax.psum_scatter(weight_acc, "space", scatter_dimension=2, tiled=True)
    return (input_acc.reshape(channels, planes, plane_len).astype(jnp.bfloat16), weight_grad)


def solution(mesh):
    return jax.shard_map(
        on_device,
        mesh=mesh,
        in_specs=(
            P("chan", "space", None),
            P("chan", "space", None),
            P("chan", "space", None),
            P(None, "chan", None),
            P("chan"),
            P("chan"),
        ),
        out_specs=(P("chan", "space", None), P(None, "chan", "space")),
        check_vma=False,
    )
```

profile of v0, /device:TPU:0, one launch (start us, length us, event | category | flops | bytes accessed | tf_op | source)
XLA Modules:
  0.0 333.1 jit_solution(11116350341319861984)
XLA Ops:
  7.2 1.0 copy.11
  8.2 5.0 %collective-permute-start.2 = (bf16[128,1,128]{0,2,1:T(8,128)(2,1)S(1)}, bf16[128,1,128]{0,2,1:T(8,128)(2,1)S(1)}, u32[]{:S(2)}, u32[]{:S(2)}) collective-permute-start(bf16[128,1,128]{0,2,1:T(8,128)(2,1)S(1)} %get-tuple-element.64), channel_id=1, source_target_pairs={{0,8},{8,16},{16,24},{1,9},{9,17},{17,25},{2,10},{10,18},{18,26},{... | collective-permute-start | bytes 98312 | tf_op jit(solution)/shard_map/ppermute | solution.py:23
  13.2 1.3 collective-permute-start.3
  14.5 1.0 copy.9
  15.5 13.0 %psum.28 = f32[128]{0:T(128)S(1)} all-reduce(f32[128]{0:T(128)S(1)} %convert_reduce_fusion), channel_id=1, replica_groups=mesh['space'=4,'chan'=8] {'space'}, use_global_device_ids=true, to_apply=%region_1.0 | all-reduce | flops 128 | bytes 1024 | tf_op jit(solution)/shard_map/psum | solution.py:59
  28.6 8.4 %psum.29 = f32[128]{0:T(128)S(1)} all-reduce(f32[128]{0:T(128)S(1)} %fusion.69), channel_id=1, replica_groups=mesh['space'=4,'chan'=8] {'space'}, use_global_device_ids=true, to_apply=%region_3.0 | all-reduce | flops 128 | bytes 1024 | tf_op jit(solution)/shard_map/psum | solution.py:61
  36.9 1.0 copy.10
  37.9 0.7 clamp_divide_fusion
  38.6 0.7 fusion.70
  39.3 10.4 %all-reduce.2 = (f32[128]{0:T(128)S(1)}, f32[128]{0:T(128)S(1)}) all-reduce(f32[128]{0:T(128)S(1)} %get-tuple-element.7, f32[128]{0:T(128)S(1)} %get-tuple-element.6), channel_id=1, replica_groups=mesh['space'=4,'chan'=8] {'space'}, use_global_device_ids=true, to_apply=%region_7.0 | all-reduce | flops 256 | bytes 2048 | tf_op jit(solution)/shard_map/psum | solution.py:64
  49.7 0.7 multiply_convert_fusion
  50.4 1.9 collective-permute-start
  52.3 1.3 collective-permute-start.1
  53.7 0.2 pad_slice_fusion.24
  53.9 4.1 %collective-permute-done.1 = bf16[128,1,128]{0,2,1:T(8,128)(2,1)S(1)} collective-permute-done((bf16[128,1,128]{0,2,1:T(8,128)(2,1)S(1)}, bf16[128,1,128]{0,2,1:T(8,128)(2,1)S(1)}, u32[]{:S(2)}, u32[]{:S(2)}) %collective-permute-start.1) | collective-permute-done | bytes 32800 | tf_op jit(solution)/shard_map/ppermute | solution.py:25
  58.1 0.7 pad_maximum_fusion
  58.8 0.1 copy.18
  58.9 0.1 copy.14
  59.0 0.1 copy.15
  59.2 0.1 copy.16
  59.3 0.1 copy.17
  59.4 0.1 copy.19
  60.5 0.1 copy.37
  60.6 0.1 copy.38
  61.0 0.1 copy.25
  61.3 0.1 copy.28
  61.4 0.1 copy.29
  61.5 0.1 copy.30
  61.9 0.1 copy.34
  62.3 18.4 %all-gather.2.cloned.1.call-done = bf16[1024,4,128]{0,2,1:T(8,128)(2,1)} async-done(((bf16[128,4,128]{0,2,1:T(8,128)(2,1)}), bf16[1024,4,128]{0,2,1:T(8,128)(2,1)}) %all-gather.2.cloned.1.call-update) | async-done | bytes 1048592 | tf_op jit(solution)/shard_map/all_gather | solution.py:75
  80.7 1.1 slice.360
  81.7 7.1 %fusion.73 = f32[27,128,1024]{2,1,0:T(8,128)} fusion(bf16[27,128,256]{2,1,0:T(8,128)(2,1)S(1)} %constant_dynamic-update-slice_fusion, bf16[1024,256,1]{0,1,2:T(8,128)(2,1)S(1)} %bitcast.221), kind=kOutput, calls=%fused_computation.186 | convolution fusion | flops 1811939328 | bytes 16449536 | tf_op jit(solution)/shard_map/kin,mn->kim/dot_general | solution.py:86
  88.8 1.2 copy-done
  90.0 0.7 pad_slice_fusion.1
  90.7 1.6 fusion.38
  92.3 3.2 pad_slice_fusion
  95.5 0.3 convolution_add_fusion.15
  95.8 0.3 convolution_add_fusion.14
  96.1 0.3 convolution_add_fusion.13
  96.4 0.3 convolution_add_fusion.12
  96.7 0.3 convolution_add_fusion.11
  97.0 0.3 convolution_add_fusion.10
  97.4 0.3 convolution_add_fusion.9
  97.7 0.3 convolution_add_fusion.8
  98.0 0.3 convolution_add_fusion.7
  98.3 0.3 convolution_add_fusion.6
  98.6 0.3 convolution_add_fusion.5
  98.9 0.3 convolution_add_fusion.4
  99.2 0.3 convolution_add_fusion.3
  99.5 0.3 convolution_add_fusion.2
  99.8 0.3 convolution_add_fusion.1
  100.1 0.3 fusion.10
  100.4 0.3 fusion.9
  100.7 0.3 fusion.8
  101.0 0.3 fusion.7
  101.3 0.3 fusion.6
  101.6 0.3 fusion.5
  101.9 0.3 fusion.4
  102.2 0.3 fusion.3
  102.5 0.3 fusion.2
  102.8 0.3 fusion.1
  103.1 0.3 fusion.11
  103.5 0.8 copy.42
  104.2 222.0 %reduce-scatter.2.cloned.1.call-done = f32[27,128,256]{2,1,0:T(8,128)} async-done(((f32[27,128,1024]{2,1,0:T(8,128)}), f32[27,128,256]{2,1,0:T(8,128)}) %reduce-scatter.2.cloned.1.call-update) | async-done | bytes 3538960 | tf_op jit(solution)/shard_map/reduce_scatter | solution.py:87
  (62 shorter events, 2.1 us)
Async XLA Ops:
  7.2 73.5 %all-gather.2.cloned.1.call-start = ((), (), s32[]{:S(2)}) async-start(), calls=%async_computation.1 | async-start | bytes 1179648 | tf_op jit(solution)/shard_map/all_gather | solution.py:75
  8.2 45.4 %collective-permute-start.2 = (bf16[128,1,128]{0,2,1:T(8,128)(2,1)S(1)}, bf16[128,1,128]{0,2,1:T(8,128)(2,1)S(1)}, u32[]{:S(2)}, u32[]{:S(2)}) collective-permute-start(bf16[128,1,128]{0,2,1:T(8,128)(2,1)S(1)} %get-tuple-element.64), channel_id=1, source_target_pairs={{0,8},{8,16},{16,24},{1,9},{9,17},{17,25},{2,10},{10,18},{18,26},{... | collective-permute-start | bytes 98312 | tf_op jit(solution)/shard_map/ppermute | solution.py:23
  13.2 40.4 %collective-permute-start.3 = (bf16[128,1,128]{0,2,1:T(8,128)(2,1)S(1)}, bf16[128,1,128]{0,2,1:T(8,128)(2,1)S(1)}, u32[]{:S(2)}, u32[]{:S(2)}) collective-permute-start(bf16[128,1,128]{0,2,1:T(8,128)(2,1)S(1)} %get-tuple-element.65), channel_id=1, source_target_pairs={{8,0},{16,8},{24,16},{9,1},{17,9},{25,17},{10,2},{18,10},{26,18},{... | collective-permute-start | bytes 98312 | tf_op jit(solution)/shard_map/ppermute | solution.py:25
  50.4 3.5 %collective-permute-start = (bf16[128,1,128]{0,2,1:T(8,128)(2,1)S(1)}, bf16[128,1,128]{0,2,1:T(8,128)(2,1)S(1)}, u32[]{:S(2)}, u32[]{:S(2)}) collective-permute-start(bf16[128,1,128]{0,2,1:T(8,128)(2,1)S(1)} %get-tuple-element.66), channel_id=1, source_target_pairs={{0,8},{8,16},{16,24},{1,9},{9,17},{17,25},{2,10},{10,18},{18,26},{... | collective-permute-start | bytes 98312 | tf_op jit(solution)/shard_map/ppermute | solution.py:23
  52.3 5.8 %collective-permute-start.1 = (bf16[128,1,128]{0,2,1:T(8,128)(2,1)S(1)}, bf16[128,1,128]{0,2,1:T(8,128)(2,1)S(1)}, u32[]{:S(2)}, u32[]{:S(2)}) collective-permute-start(bf16[128,1,128]{0,2,1:T(8,128)(2,1)S(1)} %get-tuple-element.67), channel_id=1, source_target_pairs={{8,0},{16,8},{24,16},{9,1},{17,9},{25,17},{10,2},{18,10},{26,18},{... | collective-permute-start | bytes 98312 | tf_op jit(solution)/shard_map/ppermute | solution.py:25
  58.8 267.5 %reduce-scatter.2.cloned.1.call-start = ((), (), s32[]{:S(2)}) async-start(), calls=%async_computation.2 | async-start | bytes 17694720 | tf_op jit(solution)/shard_map/reduce_scatter | solution.py:87
  88.8 1.2 copy-start
  90.0 5.5 %slice-start = ((s8[7077888]{0:T(1024)(128)(4,1)}), s8[4194304]{0:T(1024)(128)(4,1)S(1)}, s32[]{:S(2)}) async-start(s8[7077888]{0:T(1024)(128)(4,1)} %bitcast.217), calls=%async_computation.3 | async-start | bytes 8388608
  92.3 3.2 slice-start.1
Sparse Core Ops, SparseCore 0:
  58.9 21.7 all-gather.1
  88.9 237.2 reduce-scatter.1
where the time goes:
time: 334 us; the launch traced here: 333 us
  waiting for transfers between devices  245 us (73%)
  blocking collectives  31.8 us (10%)
  matrix products  16.4 us (5%)
  between operations  14.8 us (4%)
  local copies, waits for them, and re-layouts  13.2 us (4%)
  starting transfers between devices  9.49 us (3%)
    reduce_scatter x1, waiting for transfers between devices, on_device(): lax.psum_scatter(weight_acc, 'space', scatter_dimension=2, tiled=True)  222 us
    all_gather x1, waiting for transfers between devices, on_device(): full_grad = lax.all_gather(grad_rim, 'chan', axis=0, tiled=True)  18.4 us
    psum x1, blocking collectives, on_device(): mean_val = lax.psum(jnp.sum(outputs_f, axis=(1, 2)), 'space') / cells_total  13 us
    psum x1, blocking collectives, on_device(): lax.psum((jnp.sum(scaled, axis=(1, 2)), jnp.sum(scaled * normed, axis=(1,...  10.4 us
    dot_general x27, matrix products, input_terms(): jnp.dot(weight_rows[tap_index], shifted, preferred_element_type=jnp.float32)  9.35 us
    psum x1, blocking collectives, on_device(): lax.psum(jnp.sum(centred * centred, axis=(1, 2)), 'space') / cells_total  8.36 us
    dot_general x1, matrix products, on_device(): jnp.einsum('kin,mn->kim', input_shift, inner, preferred_element_type=jnp....  7.07 us
    ppermute x2, starting transfers between devices, with_halo(): lax.ppermute(tail, axis, [(i, (i + 1) % count) for i in range(ends)])  6.83 us
  transfers between devices with their start and end apart: 6, of which 3 were waited for; matrix products, arithmetic and copies ran while one was open for 6% of the time, Pallas kernels for 0%

commit v1 on v0

v1 whole, which is shorter than its diff:
```python
import functools

import jax
import jax.numpy as jnp
from jax import lax
from jax.experimental import pallas as pl
from jax.experimental.pallas import tpu as pltpu
from jax.sharding import PartitionSpec as P

H = 8
W = 16
LANES = 128

epsilon = 1e-05
clip_limit = 3.0


def exchange(ns, per, inp, conv, up, gain, sigma, ga, gb, g2, xall, sbuf, stats, *sems):
    (st_s, st_r, x_s, x_r, a_s, a_r, ap_s, ap_r, f_s, f_r, z_s, z_r, zp_s, zp_r,
     r_s, r_r, b_s, b_r, bp_s, bp_r, bf_s, bf_r) = sems
    s = lax.axis_index("space")
    c = lax.axis_index("chan")
    k = c // per
    h = c % per
    cb, pw = inp.shape
    n_local = pw

    def send(src, dst, ss, rs, sp, ch):
        copy = pltpu.make_async_remote_copy(
            src_ref=src, dst_ref=dst, send_sem=ss, recv_sem=rs,
            device_id={"space": sp, "chan": ch}, device_id_type=pl.DeviceIdType.MESH,
        )
        return copy

    barrier = pltpu.get_barrier_semaphore()
    space_peers = [lax.rem(s + e, ns) for e in range(1, ns)]
    group_peers = [lax.rem(k + d, ns) * per + h for d in range(1, ns)]
    partners = [k * per + lax.rem(h + j, per) for j in range(1, per)]
    for sp in space_peers:
        pl.semaphore_signal(barrier, inc=1, device_id={"space": sp, "chan": c}, device_id_type=pl.DeviceIdType.MESH)
    for ch in group_peers + partners:
        pl.semaphore_signal(barrier, inc=1, device_id={"space": s, "chan": ch}, device_id_type=pl.DeviceIdType.MESH)

    x = conv[...].astype(jnp.float32)
    u = up[...].astype(jnp.float32)
    m_col = jnp.sum(x, axis=1, keepdims=True) * (1.0 / n_local)
    xc = x - m_col
    m2_col = jnp.sum(xc * xc, axis=1, keepdims=True)
    su_col = jnp.sum(u, axis=1, keepdims=True)
    cux_col = jnp.sum(u * xc, axis=1, keepdims=True)
    lane = lax.broadcasted_iota(jnp.int32, (cb, LANES), 1)
    packed = jnp.where(lane == 0, m_col, jnp.where(lane == 1, m2_col, jnp.where(lane == 2, su_col, jnp.where(lane == 3, cux_col, 0.0))))
    rows = gain.shape[1]
    if rows > cb:
        packed = jnp.concatenate([packed, jnp.zeros((rows - cb, LANES), jnp.float32)], axis=0)
    flipped = packed.T[:8]
    sbuf[...] = flipped

    own_cols = pl.ds(pl.multiple_of(s * pw, LANES), pw)
    pl.semaphore_wait(barrier, 2 * (ns - 1) + per - 1)
    st_copies = [send(sbuf, stats.at[s], st_s.at[e], st_r.at[e], space_peers[e - 1], c) for e in range(1, ns)]
    for copy in st_copies:
        copy.start()
    x_copies = [send(inp, xall.at[:, own_cols], x_s.at[e], x_r.at[e], space_peers[e - 1], c) for e in range(1, ns)]
    stats[pl.ds(s, 1)] = flipped[None]
    xall[:, own_cols] = inp[...]
    for copy in st_copies:
        copy.wait_recv()

    alls = [stats[i] for i in range(ns)]
    mean = functools.reduce(lambda p, q: p + q, [t[0:1] for t in alls]) * (1.0 / ns)
    dev = [t[0:1] - mean for t in alls]
    m2 = functools.reduce(lambda p, q: p + q, [t[1:2] for t in alls])
    m2 = m2 + float(n_local) * functools.reduce(lambda p, q: p + q, [d * d for d in dev])
    cells = float(n_local * ns)
    var_eps = m2 * (1.0 / cells) + epsilon
    std = jnp.sqrt(var_eps)
    mean_up = functools.reduce(lambda p, q: p + q, [t[2:3] for t in alls]) * (1.0 / cells)
    cross = functools.reduce(lambda p, q: p + q, [t[3:4] + t[2:3] * d for t, d in zip(alls, dev)]) * (1.0 / cells)
    ratio = jnp.clip(std / sigma[...], 1.0 / clip_limit, clip_limit)
    front = ratio / std * gain[...]
    slope = cross / var_eps
    sub = lax.broadcasted_iota(jnp.int32, (LANES, rows), 0)
    coef = jnp.where(sub == 0, mean, jnp.where(sub == 1, mean_up, jnp.where(sub == 2, front, jnp.where(sub == 3, slope, 0.0))))
    coef = coef.T[:cb]
    grad = coef[:, 2:3] * (u - coef[:, 1:2] - (x - coef[:, 0:1]) * coef[:, 3:4])
    block = pl.ds(pl.multiple_of(c * cb, cb), cb)
    ga[block, :] = grad.astype(jnp.bfloat16)

    lo = pl.ds(0, LANES)
    hi = pl.ds(LANES, LANES)
    up_copy = send(ga.at[block, pl.ds(pw - LANES, LANES)], gb.at[block, lo], r_s.at[0], r_r.at[0], lax.rem(s + 1, ns), c)
    down_copy = send(ga.at[block, pl.ds(0, LANES)], gb.at[block, hi], r_s.at[1], r_r.at[1], lax.rem(s + ns - 1, ns), c)

    @pl.when(s < ns - 1)
    def _():
        up_copy.start()

    @pl.when(s > 0)
    def _():
        down_copy.start()

    a_copies = [send(ga.at[block], ga.at[block], a_s.at[d], a_r.at[d], s, group_peers[d - 1]) for d in range(1, ns)]
    ap_copies = [send(ga.at[block], ga.at[block], ap_s.at[j], ap_r.at[j], s, partners[j - 1]) for j in range(1, per)]
    for copy in a_copies + ap_copies:
        copy.start()
    for copy in x_copies:
        copy.start()

    @pl.when(s == 0)
    def _():
        gb[block, lo] = jnp.zeros((cb, LANES), jnp.bfloat16)

    @pl.when(s == ns - 1)
    def _():
        gb[block, hi] = jnp.zeros((cb, LANES), jnp.bfloat16)

    @pl.when(s > 0)
    def _():
        up_copy.wait_recv()

    @pl.when(s < ns - 1)
    def _():
        down_copy.wait_recv()

    for copy in a_copies:
        copy.wait_recv()

    def rows_of(kk, hh):
        return pl.ds(pl.multiple_of((kk * per + hh) * cb, cb), cb)

    my_rows = pl.ds(pl.multiple_of(h * cb, cb), cb)
    z_copies = [
        send(ga.at[rows_of(space_peers[e - 1], h)], g2.at[my_rows, own_cols], z_s.at[e], z_r.at[e], space_peers[e - 1], c)
        for e in range(1, ns)
    ]
    for copy in z_copies:
        copy.start()
    b_copies = [send(gb.at[block], gb.at[block], b_s.at[d], b_r.at[d], s, group_peers[d - 1]) for d in range(1, ns)]
    bp_copies = [send(gb.at[block], gb.at[block], bp_s.at[j], bp_r.at[j], s, partners[j - 1]) for j in range(1, per)]
    for copy in b_copies + bp_copies:
        copy.start()

    def forwards(ref, ss, rs):
        out = []
        for d in range(1, ns):
            piece = rows_of(lax.rem(k + ns - d, ns), h)
            for j in range(1, per):
                out.append(send(ref.at[piece], ref.at[piece], ss.at[d, j], rs.at[d, j], s, partners[j - 1]))
        return out

    f_copies = forwards(ga, f_s, f_r)
    for copy in f_copies:
        copy.start()
    for copy in b_copies:
        copy.wait_recv()
    bf_copies = forwards(gb, bf_s, bf_r)
    for copy in bf_copies:
        copy.start()
    zp_copies = []
    for e in range(1, ns):
        z_copies[e - 1].wait_recv()
        cols = pl.ds(pl.multiple_of(lax.rem(s + ns - e, ns) * pw, LANES), pw)
        for j in range(1, per):
            copy = send(g2.at[my_rows, cols], g2.at[my_rows, cols], zp_s.at[e, j], zp_r.at[e, j], s, partners[j - 1])
            copy.start()
            zp_copies.append(copy)
    for copy in ap_copies + f_copies:
        copy.wait_recv()
    g2[:, own_cols] = ga[pl.ds(pl.multiple_of(s * (per * cb), per * cb), per * cb), :]
    for copy in x_copies + bp_copies + bf_copies + zp_copies:
        copy.wait_recv()
    for copy in st_copies + x_copies + a_copies + ap_copies + f_copies + z_copies + zp_copies + b_copies + bp_copies + bf_copies:
        copy.wait_send()

    @pl.when(s < ns - 1)
    def _():
        up_copy.wait_send()

    @pl.when(s > 0)
    def _():
        down_copy.wait_send()


def moved(plane, row_off, col_off, sign):
    row_off, col_off = sign * row_off, sign * col_off
    delta = row_off * W + col_off
    if delta == 0:
        return plane
    width = plane.shape[1]
    out = pltpu.roll(plane, (-delta) % width, 1)
    cell = lax.broadcasted_iota(jnp.int32, plane.shape, 1)
    row = cell // W + row_off
    col = cell % W + col_off
    return jnp.where((row >= 0) & (row < H) & (col >= 0) & (col < W), out, 0.0)


def products(ns, w, ga, gb, g2, xall, ig, wg, gp, xs, acc):
    a = pl.program_id(0)
    cb, total = xall.shape
    pw = ga.shape[1]
    planes = pw // LANES
    depth = total // LANES

    @pl.when(a == 0)
    def _():
        gp[:, 0:LANES] = gb[:, 0:LANES]
        gp[:, LANES : LANES + pw] = ga[...]
        gp[:, LANES + pw :] = gb[:, LANES:]
        zero = jnp.zeros((9 * cb, LANES), jnp.bfloat16)
        xs[:, 0:LANES] = zero
        xs[:, LANES + total :] = zero
        for d in range(depth):
            plane = xall[:, d * LANES : (d + 1) * LANES].astype(jnp.float32)
            for b in range(3):
                for e in range(3):
                    at = (3 * b + e) * cb
                    xs[at : at + cb, (d + 1) * LANES : (d + 2) * LANES] = moved(plane, b - 1, e - 1, 1).astype(jnp.bfloat16)

    shifted = xs[:, pl.ds(pl.multiple_of(a * LANES, LANES), total)]
    wgrad = lax.dot_general(shifted, g2[...], (((1,), (1,)), ((), ())), preferred_element_type=jnp.float32)
    wg[...] = wgrad.reshape(wg.shape)
    rhs = gp[:, pl.ds(pl.multiple_of((2 - a) * LANES, LANES), pw)]
    part = jnp.dot(w[...].reshape(9 * cb, w.shape[2]), rhs, preferred_element_type=jnp.float32)

    @pl.when(a == 0)
    def _():
        acc[...] = part

    @pl.when(a > 0)
    def _():
        acc[...] += part

    @pl.when(a == 2)
    def _():
        for p in range(planes):
            out = jnp.zeros((cb, LANES), jnp.float32)
            for b in range(3):
                for e in range(3):
                    at = (3 * b + e) * cb
                    out = out + moved(acc[at : at + cb, p * LANES : (p + 1) * LANES], b - 1, e - 1, -1)
            ig[:, p * LANES : (p + 1) * LANES] = out.astype(jnp.bfloat16)


def solution(mesh):
    ns = mesh.shape["space"]
    nc = mesh.shape["chan"]
    per = nc // ns

    def on_device(inputs, conv_out, upstream, weights, norm_gain, run_sigma):
        cb, planes, plane_len = inputs.shape
        pw = planes * plane_len
        channels = cb * nc
        rows = max(cb, LANES)

        def flat(t):
            return t.reshape(cb, pw)

        def row(t):
            return jnp.pad(t, (0, rows - cb), constant_values=1.0).reshape(1, rows)

        vmem = pl.BlockSpec(memory_space=pltpu.VMEM)
        dma = pltpu.SemaphoreType.DMA
        sem_shapes = []
        for shape in ((ns,), (ns,), (ns,), (per,), (ns, per), (ns,), (ns, per), (2,), (ns,), (per,), (ns, per)):
            sem_shapes += [dma(shape), dma(shape)]
        bf = jnp.bfloat16
        ga, gb, g2, xall = pl.pallas_call(
            functools.partial(exchange, ns, per),
            out_shape=(
                jax.ShapeDtypeStruct((channels, pw), bf),
                jax.ShapeDtypeStruct((channels, 2 * LANES), bf),
                jax.ShapeDtypeStruct((per * cb, ns * pw), bf),
                jax.ShapeDtypeStruct((cb, ns * pw), bf),
            ),
            in_specs=[vmem] * 5,
            out_specs=(vmem,) * 4,
            scratch_shapes=[pltpu.VMEM((8, rows), jnp.float32), pltpu.VMEM((ns, 8, rows), jnp.float32)] + sem_shapes,
            compiler_params=pltpu.CompilerParams(collective_id=0, has_side_effects=True),
        )(flat(inputs), flat(conv_out), flat(upstream), row(norm_gain), row(run_sigma))

        ig, wg = pl.pallas_call(
            functools.partial(products, ns),
            grid=(3,),
            out_shape=(
                jax.ShapeDtypeStruct((cb, pw), bf),
                jax.ShapeDtypeStruct((27, cb, per * cb), jnp.float32),
            ),
            in_specs=[
                pl.BlockSpec((9, cb, channels), lambda a: (a, 0, 0)),
                vmem, vmem, vmem, vmem,
            ],
            out_specs=(
                pl.BlockSpec((cb, pw), lambda a: (0, 0)),
                pl.BlockSpec((9, cb, per * cb), lambda a: (a, 0, 0)),
            ),
            scratch_shapes=[
                pltpu.VMEM((channels, pw + 2 * LANES), bf),
                pltpu.VMEM((9 * cb, ns * pw + 2 * LANES), bf),
                pltpu.VMEM((9 * cb, pw), jnp.float32),
            ],
        )(weights, ga, gb, g2, xall)
        return ig.reshape(cb, planes, plane_len), wg

    return jax.shard_map(
        on_device,
        mesh=mesh,
        in_specs=(
            P("chan", "space", None),
            P("chan", "space", None),
            P("chan", "space", None),
            P(None, "chan", None),
            P("chan"),
            P("chan"),
        ),
        out_specs=(P("chan", "space", None), P(None, "chan", "space")),
        check_vma=False,
    )
```

time: 334 us -> 39.8 us (0.12)
  waiting for transfers between devices: 245 us -> 0 us
  Pallas kernels: 0 us -> 34.3 us
  blocking collectives: 31.8 us -> 0 us
  matrix products: 16.4 us -> 0 us
  between operations: 14.8 us -> 0.64 us
  starting transfers between devices: 9.49 us -> 0 us
  local copies, waits for them, and re-layouts: 13.2 us -> 4.5 us
    reduce_scatter x1 -> x0, waiting for transfers between devices: 222 us -> none  [on_device(): lax.psum_scatter(weight_acc, 'space', scatter_dimension=2, tiled=True)]
    pallas_call x0 -> x2, Pallas kernels: none -> 34.3 us  [the longest x1 24.9 us: on_device(): pl.pallas_call(functools.partial(exchange, ns, per), out_shape=(jax.Shape...]
    psum x3 -> x0, blocking collectives: 31.8 us -> none  [the longest x1 13 us: on_device(): mean_val = lax.psum(jnp.sum(outputs_f, axis=(1, 2)), 'space') / cells_total]
    all_gather x1 -> x0, waiting for transfers between devices: 18.4 us -> none  [on_device(): full_grad = lax.all_gather(grad_rim, 'chan', axis=0, tiled=True)]
    dot_general x28 -> x0, matrix products: 16.4 us -> none  [the longest x27 9.35 us: input_terms(): jnp.dot(weight_rows[tap_index], shifted, preferred_element_type=jnp.float32)]
    ppermute x4 -> x0, starting transfers between devices: 9.41 us -> none  [the longest x2 6.83 us: with_halo(): lax.ppermute(tail, axis, [(i, (i + 1) % count) for i in range(ends)])]
    slice x7 -> x0, local copies, waits for them, and re-layouts: 5.21 us -> none  [the longest x4 4.12 us: tap_cut(): padded[:, depth_from:depth_from + planes, row_from:row_from + H, col_from...]
    ppermute x4 -> x0, waiting for transfers between devices: 4.16 us -> none  [the longest x2 4.15 us: with_halo(): lax.ppermute(head, axis, [((i + 1) % count, i) for i in range(ends)])]
  transfers between devices with their start and end apart: 6 -> 0, of which waited for: 3 -> 0; matrix products, arithmetic and copies ran while one was open for 6% -> 0% of each run, Pallas kernels for 0% -> 0%
where the time goes in v1:
time: 39.8 us; the launch traced here: 39.4 us
  Pallas kernels  34.3 us (86%)
  local copies, waits for them, and re-layouts  4.5 us (11%)
  between operations  0.64 us (2%)
    pallas_call x1, Pallas kernels, on_device(): pl.pallas_call(functools.partial(exchange, ns, per), out_shape=(jax.Shape...  24.9 us
    pallas_call x1, Pallas kernels, on_device(): pl.pallas_call(functools.partial(products, ns), grid=(3,), out_shape=(jax...  9.42 us
    reshape x1, local copies, waits for them, and re-layouts, flat(): return t.reshape(cb, pw)  1.53 us
    reshape x1, local copies, waits for them, and re-layouts, on_device(): return (ig.reshape(cb, planes, plane_len), wg)  1.49 us
    unnamed x1, local copies, waits for them, and re-layouts  1.48 us

profile of v1, /device:TPU:0, one launch (start us, length us, event | category | flops | bytes accessed | tf_op | source)
XLA Modules:
  0.0 39.4 jit_solution(2867298404016889632)
XLA Ops:
  0.6 1.5 %copy.14 = bf16[16,8,2,128]{3,1,2,0:T(8,128)(2,1)} copy(bf16[16,8,2,128]{3,2,1,0:T(2,128)(2,1)} %bitcast.13) | data formatting | bytes 131072
  2.1 1.5 %copy_bitcast_fusion = (bf16[128,256]{1,0:T(8,128)(2,1)}, bf16[128,256]{1,0:T(8,128)(2,1)}) fusion(bf16[16,8,2,128]{3,2,1,0:T(2,128)(2,1)} %bitcast.14, bf16[16,8,2,128]{3,2,1,0:T(2,128)(2,1)} %bitcast.15), kind=kLoop, calls=%fused_computation | loop fusion | bytes 262144 | tf_op jit(solution)/shard_map/reshape | solution.py:257
  3.6 24.9 %shard_map.77 = (bf16[1024,256]{1,0:T(8,128)(2,1)}, bf16[1024,256]{1,0:T(8,128)(2,1)}, bf16[256,1024]{1,0:T(8,128)(2,1)}, bf16[128,1024]{1,0:T(8,128)(2,1)}) custom-call(bf16[128,256]{1,0:T(8,128)(2,1)} %bitcast.12, bf16[128,256]{1,0:T(8,128)(2,1)} %get-tuple-element.15.conv, bf16[128,256]{1,0:T(8,128)(2,1)} %get-tuple-element.14.up, f32[1,128]{1,0:T(1,128)} %bitcast.16, ...), custom_call_target="tpu_custom_call" | custom-call | tf_op jit(solution)/shard_map/pallas_call | solution.py:268
  28.5 9.4 %shard_map.78 = (bf16[128,256]{1,0:T(8,128)(2,1)}, f32[27,128,256]{2,1,0:T(8,128)}) custom-call(bf16[27,128,1024]{2,1,0:T(8,128)(2,1)} %w.1, bf16[1024,256]{1,0:T(8,128)(2,1)} %get-tuple-element.8.ga, bf16[1024,256]{1,0:T(8,128)(2,1)} %get-tuple-element.9.gb, bf16[256,1024]{1,0:T(8,128)(2,1)} %get-tuple-element.10.g2, bf16[128,1024]{1,0:T(8,128)(2,1)} %get-tuple-element.11.xall), custom_call_target="tpu_custom_call" | custom-call | tf_op jit(solution)/shard_map/pallas_call | solution.py:282
  37.9 1.5 %reshape.27 = bf16[128,2,128]{2,1,0:T(2,128)(2,1)} reshape(bf16[128,256]{1,0:T(8,128)(2,1)} %get-tuple-element.12) | data formatting | bytes 131072 | tf_op jit(solution)/shard_map/reshape | solution.py:303

commit v2 on v1

--- a/solution.py
+++ b/solution.py
@@ -15,15 +15,23 @@
 clip_limit = 3.0
 
 
-def exchange(ns, per, inp, conv, up, gain, sigma, ga, gb, g2, xall, sbuf, stats, *sems):
+def planes_flat(ref):
+    return jnp.concatenate([ref[:, p, :].astype(jnp.float32) for p in range(ref.shape[1])], axis=1)
+
+
+def exchange(ns, per, inp, conv, up, gain, sigma, w, ig, g2, xall, ga, gb, sbuf, stats, xbuf, wbuf, acc, w_sem, *sems):
     (st_s, st_r, x_s, x_r, a_s, a_r, ap_s, ap_r, f_s, f_r, z_s, z_r, zp_s, zp_r,
      r_s, r_r, b_s, b_r, bp_s, bp_r, bf_s, bf_r) = sems
     s = lax.axis_index("space")
     c = lax.axis_index("chan")
     k = c // per
     h = c % per
-    cb, pw = inp.shape
+    cb, planes, _ = inp.shape
+    pw = planes * LANES
     n_local = pw
+    w_copies = [pltpu.make_async_copy(w.at[pl.ds(9 * a, 9)], wbuf.at[pl.ds(9 * a, 9)], w_sem.at[a]) for a in (1, 2, 0)]
+    for copy in w_copies:
+        copy.start()
 
     def send(src, dst, ss, rs, sp, ch):
         copy = pltpu.make_async_remote_copy(
@@ -41,8 +49,9 @@
     for ch in group_peers + partners:
         pl.semaphore_signal(barrier, inc=1, device_id={"space": s, "chan": ch}, device_id_type=pl.DeviceIdType.MESH)
 
-    x = conv[...].astype(jnp.float32)
-    u = up[...].astype(jnp.float32)
+    x = planes_flat(conv)
+    u = planes_flat(up)
+    xbuf[...] = planes_flat(inp).astype(jnp.bfloat16)
     m_col = jnp.sum(x, axis=1, keepdims=True) * (1.0 / n_local)
     xc = x - m_col
     m2_col = jnp.sum(xc * xc, axis=1, keepdims=True)
@@ -61,9 +70,11 @@
     st_copies = [send(sbuf, stats.at[s], st_s.at[e], st_r.at[e], space_peers[e - 1], c) for e in range(1, ns)]
     for copy in st_copies:
         copy.start()
-    x_copies = [send(inp, xall.at[:, own_cols], x_s.at[e], x_r.at[e], space_peers[e - 1], c) for e in range(1, ns)]
+    x_copies = [send(xbuf, xall.at[:, own_cols], x_s.at[e], x_r.at[e], space_peers[e - 1], c) for e in range(1, ns)]
+    for copy in x_copies:
+        copy.start()
     stats[pl.ds(s, 1)] = flipped[None]
-    xall[:, own_cols] = inp[...]
+    xall[:, own_cols] = xbuf[...]
     for copy in st_copies:
         copy.wait_recv()
 
@@ -104,8 +115,6 @@
     ap_copies = [send(ga.at[block], ga.at[block], ap_s.at[j], ap_r.at[j], s, partners[j - 1]) for j in range(1, per)]
     for copy in a_copies + ap_copies:
         copy.start()
-    for copy in x_copies:
-        copy.start()
 
     @pl.when(s == 0)
     def _():
@@ -123,6 +132,10 @@
     def _():
         down_copy.wait_recv()
 
+    b_copies = [send(gb.at[block], gb.at[block], b_s.at[d], b_r.at[d], s, group_peers[d - 1]) for d in range(1, ns)]
+    bp_copies = [send(gb.at[block], gb.at[block], bp_s.at[j], bp_r.at[j], s, partners[j - 1]) for j in range(1, per)]
+    for copy in b_copies + bp_copies:
+        copy.start()
     for copy in a_copies:
         copy.wait_recv()
 
@@ -136,11 +149,6 @@
     ]
     for copy in z_copies:
         copy.start()
-    b_copies = [send(gb.at[block], gb.at[block], b_s.at[d], b_r.at[d], s, group_peers[d - 1]) for d in range(1, ns)]
-    bp_copies = [send(gb.at[block], gb.at[block], bp_s.at[j], bp_r.at[j], s, partners[j - 1]) for j in range(1, per)]
-    for copy in b_copies + bp_copies:
-        copy.start()
-
     def forwards(ref, ss, rs):
         out = []
         for d in range(1, ns):
@@ -152,11 +160,29 @@
     f_copies = forwards(ga, f_s, f_r)
     for copy in f_copies:
         copy.start()
+    def product(a, rhs):
+        w_copies[(a + 2) % 3].wait()
+        taps = wbuf[9 * a : 9 * a + 9].reshape(9 * cb, wbuf.shape[2])
+        return jnp.dot(taps, rhs, preferred_element_type=jnp.float32)
+
+    for copy in ap_copies + f_copies:
+        copy.wait_recv()
+    acc[...] = product(1, ga[...])
     for copy in b_copies:
         copy.wait_recv()
     bf_copies = forwards(gb, bf_s, bf_r)
     for copy in bf_copies:
         copy.start()
+    g2[:, own_cols] = ga[pl.ds(pl.multiple_of(s * (per * cb), per * cb), per * cb), :]
+    for copy in bp_copies + bf_copies:
+        copy.wait_recv()
+    if planes > 1:
+        below = jnp.concatenate([gb[:, 0:LANES], ga[:, 0 : pw - LANES]], axis=1)
+        above = jnp.concatenate([ga[:, LANES:], gb[:, LANES:]], axis=1)
+    else:
+        below, above = gb[:, 0:LANES], gb[:, LANES:]
+    acc[...] += product(2, below)
+    acc[...] += product(0, above)
     zp_copies = []
     for e in range(1, ns):
         z_copies[e - 1].wait_recv()
@@ -165,10 +191,14 @@
             copy = send(g2.at[my_rows, cols], g2.at[my_rows, cols], zp_s.at[e, j], zp_r.at[e, j], s, partners[j - 1])
             copy.start()
             zp_copies.append(copy)
-    for copy in ap_copies + f_copies:
-        copy.wait_recv()
-    g2[:, own_cols] = ga[pl.ds(pl.multiple_of(s * (per * cb), per * cb), per * cb), :]
-    for copy in x_copies + bp_copies + bf_copies + zp_copies:
+    for p in range(planes):
+        out = jnp.zeros((cb, LANES), jnp.float32)
+        for b in range(3):
+            for e in range(3):
+                at = (3 * b + e) * cb
+                out = out + moved(acc[at : at + cb, p * LANES : (p + 1) * LANES], b - 1, e - 1, -1)
+        ig[:, p * LANES : (p + 1) * LANES] = out.astype(jnp.bfloat16)
+    for copy in x_copies + zp_copies:
         copy.wait_recv()
     for copy in st_copies + x_copies + a_copies + ap_copies + f_copies + z_copies + zp_copies + b_copies + bp_copies + bf_copies:
         copy.wait_send()
@@ -195,18 +225,13 @@
     return jnp.where((row >= 0) & (row < H) & (col >= 0) & (col < W), out, 0.0)
 
 
-def products(ns, w, ga, gb, g2, xall, ig, wg, gp, xs, acc):
+def products(ig_flat, g2, xall, ig, wg, xs):
     a = pl.program_id(0)
     cb, total = xall.shape
-    pw = ga.shape[1]
-    planes = pw // LANES
     depth = total // LANES
 
     @pl.when(a == 0)
     def _():
-        gp[:, 0:LANES] = gb[:, 0:LANES]
-        gp[:, LANES : LANES + pw] = ga[...]
-        gp[:, LANES + pw :] = gb[:, LANES:]
         zero = jnp.zeros((9 * cb, LANES), jnp.bfloat16)
         xs[:, 0:LANES] = zero
         xs[:, LANES + total :] = zero
@@ -216,30 +241,13 @@
                 for e in range(3):
                     at = (3 * b + e) * cb
                     xs[at : at + cb, (d + 1) * LANES : (d + 2) * LANES] = moved(plane, b - 1, e - 1, 1).astype(jnp.bfloat16)
+        planes = ig.shape[1]
+        cols = [ig_flat[:, p * LANES : (p + 1) * LANES].astype(jnp.float32) for p in range(planes)]
+        ig[...] = jnp.stack(cols, axis=1).astype(jnp.bfloat16)
 
     shifted = xs[:, pl.ds(pl.multiple_of(a * LANES, LANES), total)]
     wgrad = lax.dot_general(shifted, g2[...], (((1,), (1,)), ((), ())), preferred_element_type=jnp.float32)
     wg[...] = wgrad.reshape(wg.shape)
-    rhs = gp[:, pl.ds(pl.multiple_of((2 - a) * LANES, LANES), pw)]
-    part = jnp.dot(w[...].reshape(9 * cb, w.shape[2]), rhs, preferred_element_type=jnp.float32)
-
-    @pl.when(a == 0)
-    def _():
-        acc[...] = part
-
-    @pl.when(a > 0)
-    def _():
-        acc[...] += part
-
-    @pl.when(a == 2)
-    def _():
-        for p in range(planes):
-            out = jnp.zeros((cb, LANES), jnp.float32)
-            for b in range(3):
-                for e in range(3):
-                    at = (3 * b + e) * cb
-                    out = out + moved(acc[at : at + cb, p * LANES : (p + 1) * LANES], b - 1, e - 1, -1)
-            ig[:, p * LANES : (p + 1) * LANES] = out.astype(jnp.bfloat16)
 
 
 def solution(mesh):
@@ -252,9 +260,6 @@
         pw = planes * plane_len
         channels = cb * nc
         rows = max(cb, LANES)
-
-        def flat(t):
-            return t.reshape(cb, pw)
 
         def row(t):
             return jnp.pad(t, (0, rows - cb), constant_values=1.0).reshape(1, rows)
@@ -265,42 +270,43 @@
         for shape in ((ns,), (ns,), (ns,), (per,), (ns, per), (ns,), (ns, per), (2,), (ns,), (per,), (ns, per)):
             sem_shapes += [dma(shape), dma(shape)]
         bf = jnp.bfloat16
-        ga, gb, g2, xall = pl.pallas_call(
+        ig_flat, g2, xall = pl.pallas_call(
             functools.partial(exchange, ns, per),
             out_shape=(
-                jax.ShapeDtypeStruct((channels, pw), bf),
-                jax.ShapeDtypeStruct((channels, 2 * LANES), bf),
+                jax.ShapeDtypeStruct((cb, pw), bf),
                 jax.ShapeDtypeStruct((per * cb, ns * pw), bf),
                 jax.ShapeDtypeStruct((cb, ns * pw), bf),
             ),
-            in_specs=[vmem] * 5,
-            out_specs=(vmem,) * 4,
-            scratch_shapes=[pltpu.VMEM((8, rows), jnp.float32), pltpu.VMEM((ns, 8, rows), jnp.float32)] + sem_shapes,
+            in_specs=[vmem] * 5 + [pl.BlockSpec(memory_space=pl.ANY)],
+            out_specs=(vmem,) * 3,
+            scratch_shapes=[
+                pltpu.VMEM((channels, pw), bf),
+                pltpu.VMEM((channels, 2 * LANES), bf),
+                pltpu.VMEM((8, rows), jnp.float32),
+                pltpu.VMEM((ns, 8, rows), jnp.float32),
+                pltpu.VMEM((cb, pw), bf),
+                pltpu.VMEM(weights.shape, bf),
+                pltpu.VMEM((9 * cb, pw), jnp.float32),
+                dma((3,)),
+            ] + sem_shapes,
             compiler_params=pltpu.CompilerParams(collective_id=0, has_side_effects=True),
-        )(flat(inputs), flat(conv_out), flat(upstream), row(norm_gain), row(run_sigma))
+        )(inputs, conv_out, upstream, row(norm_gain), row(run_sigma), weights)
 
         ig, wg = pl.pallas_call(
-            functools.partial(products, ns),
+            products,
             grid=(3,),
             out_shape=(
-                jax.ShapeDtypeStruct((cb, pw), bf),
+                jax.ShapeDtypeStruct(inputs.shape, bf),
                 jax.ShapeDtypeStruct((27, cb, per * cb), jnp.float32),
             ),
-            in_specs=[
-                pl.BlockSpec((9, cb, channels), lambda a: (a, 0, 0)),
-                vmem, vmem, vmem, vmem,
-            ],
+            in_specs=[vmem, vmem, vmem],
             out_specs=(
-                pl.BlockSpec((cb, pw), lambda a: (0, 0)),
+                pl.BlockSpec(inputs.shape, lambda a: (0, 0, 0)),
                 pl.BlockSpec((9, cb, per * cb), lambda a: (a, 0, 0)),
             ),
-            scratch_shapes=[
-                pltpu.VMEM((channels, pw + 2 * LANES), bf),
-                pltpu.VMEM((9 * cb, ns * pw + 2 * LANES), bf),
-                pltpu.VMEM((9 * cb, pw), jnp.float32),
-            ],
-        )(weights, ga, gb, g2, xall)
-        return ig.reshape(cb, planes, plane_len), wg
+            scratch_shapes=[pltpu.VMEM((9 * cb, ns * pw + 2 * LANES), bf)],
+        )(ig_flat, g2, xall)
+        return ig, wg
 
     return jax.shard_map(
         on_device,

time: 39.8 us -> 31.1 us (0.78)
  local copies, waits for them, and re-layouts: 4.5 us -> 0 us
  Pallas kernels: 34.3 us -> 30.2 us
    pallas_call x1, Pallas kernels: 9.42 us -> 5.62 us  [on_device(): pl.pallas_call(products, grid=(3,), out_shape=(jax.ShapeDtypeStruct(input...]
    reshape x2 -> x0, local copies, waits for them, and re-layouts: 3.02 us -> none  [the longest x1 1.53 us: flat(): return t.reshape(cb, pw)]
    unnamed x1 -> x0, local copies, waits for them, and re-layouts: 1.48 us -> none
where the time goes in v2:
time: 31.1 us; the launch traced here: 30.9 us
  Pallas kernels  30.2 us (97%)
  between operations  0.64 us (2%)
    pallas_call x1, Pallas kernels, on_device(): pl.pallas_call(functools.partial(exchange, ns, per), out_shape=(jax.Shape...  24.6 us
    pallas_call x1, Pallas kernels, on_device(): pl.pallas_call(products, grid=(3,), out_shape=(jax.ShapeDtypeStruct(input...  5.62 us

profile of v2, /device:TPU:0, one launch (start us, length us, event | category | flops | bytes accessed | tf_op | source)
XLA Modules:
  0.0 30.9 jit_solution(17771358282721224794)
XLA Ops:
  0.6 24.6 %shard_map.77 = (bf16[128,256]{1,0:T(8,128)(2,1)}, bf16[256,1024]{1,0:T(8,128)(2,1)}, bf16[128,1024]{1,0:T(8,128)(2,1)}) custom-call(bf16[128,2,128]{2,1,0:T(2,128)(2,1)} %inp.1, bf16[128,2,128]{2,1,0:T(2,128)(2,1)} %conv.1, bf16[128,2,128]{2,1,0:T(2,128)(2,1)} %up.1, f32[1,128]{1,0:T(1,128)} %bitcast.2, f32[1,128]{1,0:T(1,128)} %bitcast.3, ...), custom_call_target="tpu_custom_call" | custom-call | tf_op jit(solution)/shard_map/pallas_call | solution.py:273
  25.3 5.6 %shard_map.78 = (bf16[128,2,128]{2,1,0:T(2,128)(2,1)}, f32[27,128,256]{2,1,0:T(8,128)}) custom-call(bf16[128,256]{1,0:T(8,128)(2,1)} %get-tuple-element.5.ig_flat, bf16[256,1024]{1,0:T(8,128)(2,1)} %get-tuple-element.6.g2, bf16[128,1024]{1,0:T(8,128)(2,1)} %get-tuple-element.7.xall), custom_call_target="tpu_custom_call" | custom-call | tf_op jit(solution)/shard_map/pallas_call | solution.py:295
